TPU v7x, 128 devices: a whole 4x4x4 slice. The times are simulated.
128 devices in a mesh: row: 8 (over z, core), col: 16 (over y, x).
Axes of the slice: x: 4, y: 4, z: 4, core: 2. Of those that a mesh axis runs over, the one named last changes fastest.
Arguments:
- kernel: float32 [16384, 16384], P('row', 'col'), may hold values from 0 to 3, as said below
Outputs:
- trailing: float32 [16384, 16384], P('row', 'col')
- factor_t: float32 [1024, 16384], P('col', 'row')
Inputs may be any that keep to these rules, and one draw needn't show every extreme that they name: K is symmetric: an RBF kernel over 256 donor features plus each donor's noise variance, of 0.5 or more, on the diagonal.
All inputs are finite; a program needn't handle non-finite values.
Results may differ from a plain program's by a relative error of at most 0.0003.
Values sent between devices are 32-bit elements; how exact they have to be, the bound alone decides.
A program may use at most 128 MiB of HBM per device.

v0:
```python
import jax
import jax.numpy as jnp
from jax import lax
from jax.sharding import PartitionSpec as P

PANEL = 512
PANELS = 2


def from_root(value, axis, source):
    kept = jnp.where(lax.axis_index(axis) == source, value, 0).astype(value.dtype)
    return lax.psum(kept, axis)


def outer_update(left_fac, right_fac):
    return lax.dot_general(
        left_fac,
        right_fac,
        (((0,), (0,)), ((), ())),
        precision=lax.Precision.HIGHEST,
        preferred_element_type=jnp.float32,
    )


def local(kernel):
    grid_rows = lax.axis_size("row")
    grid_cols = lax.axis_size("col")
    my_row = lax.axis_index("row")
    my_col = lax.axis_index("col")
    rows_loc = kernel.shape[0]
    cols_loc = kernel.shape[1]
    tile_w = PANEL // grid_cols
    spread = grid_cols // grid_rows
    row_local = jnp.arange(rows_loc, dtype=jnp.int32)
    row_ids = (row_local // tile_w * grid_rows + my_row) * tile_w + row_local % tile_w
    col_local = jnp.arange(cols_loc, dtype=jnp.int32)
    col_ids = (col_local // tile_w * grid_cols + my_col) * tile_w + col_local % tile_w
    down_list = []
    schur = kernel
    for panel_idx in range(PANELS):
        column_tile = schur[:, panel_idx * tile_w : (panel_idx + 1) * tile_w]
        first_col = panel_idx * PANEL
        first_tile = panel_idx * spread
        corner = column_tile[first_tile * tile_w : (first_tile + spread) * tile_w]
        flat_block = corner.reshape(1, spread * tile_w * tile_w)
        blocks = lax.all_gather(flat_block, ("row", "col"), axis=0, tiled=True)
        blocks = blocks.reshape(grid_rows, grid_cols, spread, tile_w, tile_w)
        blocks = blocks.transpose(2, 0, 3, 1, 4).reshape(PANEL, PANEL)
        lower_fac = jnp.linalg.cholesky(blocks)
        columns_t = column_tile.T
        gathered = lax.all_gather(columns_t, "col", axis=0, tiled=True)
        factor_loc = jax.scipy.linalg.solve_triangular(lower_fac, gathered, lower=True)
        factor_loc = jnp.where(row_ids[None, :] >= first_col, factor_loc, 0.0)
        picked = factor_loc.reshape(PANEL, cols_loc // tile_w, spread, tile_w)
        picked = lax.dynamic_index_in_dim(picked, my_col // grid_rows, 2, keepdims=False)
        picked = picked.reshape(PANEL, cols_loc)
        across = from_root(picked, "row", my_col % grid_rows)
        factor_loc, across = (factor_loc, across)
        schur = schur - outer_update(factor_loc, across)
        down_list.append(factor_loc)
    limit = PANELS * PANEL
    keep = (row_ids[:, None] >= limit) & (col_ids[None, :] >= limit)
    trailing = jnp.where(keep, schur, 0.0)
    stacked = jnp.concatenate(down_list, axis=0)
    per_col = PANELS * PANEL // grid_cols
    factor_out = lax.dynamic_slice_in_dim(stacked, my_col * per_col, per_col, 0)
    return (trailing, factor_out)


def solution(mesh):
    return jax.shard_map(
        local,
        mesh=mesh,
        in_specs=(P("row", "col"),),
        out_specs=(P("row", "col"), P("col", "row")),
        check_vma=False,
    )
```

profile of v0, /device:TPU:0, one launch (start us, length us, event | category | flops | bytes accessed | tf_op | source)
XLA Modules:
  0.0 662.9 jit_solution(6436545868017596230)
XLA Ops:
  8.7 9.1 %copy.22 = f32[2048,1024]{0,1:T(8,128)} copy(f32[2048,1024]{1,0:T(8,128)} %param.4) | data formatting | bytes 16777216 | tf_op args[0]
  19.7 57.2 %all-gather.11.cloned.1.call-done = f32[128,1,2048]{2,1,0:T(1,128)} async-done(((f32[1,1,2048]{2,1,0:T(1,128)}), f32[128,1,2048]{2,1,0:T(1,128)}) %all-gather.11.cloned.1.call-update) | async-done | bytes 1048592 | tf_op jit(solution)/shard_map/all_gather | solution.py:46
  93.2 11.7 %cholesky.286 = f32[128,128]{1,0:T(8,128)S(1)} custom-call(f32[128,128]{1,0:T(8,128)S(1)} %cholesky.426), custom_call_target="Cholesky" | custom-call | tf_op jit(solution)/shard_map/jit(cholesky)/cholesky | solution.py:49
  105.0 9.8 %custom-call.27 = f32[1,128,128]{1,2,0:T(8,128)S(1)} custom-call(f32[1,128,128]{2,1,0:T(8,128)S(1)} %get-tuple-element.65), custom_call_target="InvertDiagBlocksLowerTriangular" | custom-call | tf_op jit(solution)/shard_map/jit(cholesky)/cholesky | solution.py:49
  115.6 11.7 %cholesky.305 = f32[128,128]{1,0:T(8,128)S(1)} custom-call(f32[128,128]{1,0:T(8,128)S(1)} %cholesky.430), custom_call_target="Cholesky" | custom-call | tf_op jit(solution)/shard_map/jit(cholesky)/cholesky | solution.py:49
  127.3 10.0 %custom-call.28 = f32[1,128,128]{1,2,0:T(8,128)S(1)} custom-call(f32[1,128,128]{2,1,0:T(8,128)S(1)} %get-tuple-element.62), custom_call_target="InvertDiagBlocksLowerTriangular" | custom-call | tf_op jit(solution)/shard_map/jit(cholesky)/cholesky | solution.py:49
  138.0 11.7 %cholesky.326 = f32[128,128]{1,0:T(8,128)S(1)} custom-call(f32[128,128]{1,0:T(8,128)S(1)} %cholesky.435), custom_call_target="Cholesky" | custom-call | tf_op jit(solution)/shard_map/jit(cholesky)/cholesky | solution.py:49
  149.7 9.8 %custom-call.29 = f32[1,128,128]{1,2,0:T(8,128)S(1)} custom-call(f32[1,128,128]{2,1,0:T(8,128)S(1)} %get-tuple-element.59), custom_call_target="InvertDiagBlocksLowerTriangular" | custom-call | tf_op jit(solution)/shard_map/jit(cholesky)/cholesky | solution.py:49
  160.2 11.7 %cholesky.343 = f32[128,128]{1,0:T(8,128)S(1)} custom-call(f32[128,128]{1,0:T(8,128)S(1)} %convolution_subtract_fusion.10), custom_call_target="Cholesky" | custom-call | tf_op jit(solution)/shard_map/jit(cholesky)/cholesky | solution.py:49
  184.8 39.3 %custom-call.30 = f32[4,128,128]{1,2,0:T(8,128)S(1)} custom-call(f32[4,128,128]{2,1,0:T(8,128)S(1)} %get-tuple-element.18), custom_call_target="InvertDiagBlocksLowerTriangular" | custom-call | tf_op jit(solution)/shard_map/jit(_solve_triangular)/triangular_solve | solution.py:52
  246.5 63.6 %all-reduce.4.cloned.1.call-done = f32[512,1024]{0,1:T(8,128)} async-done(((f32[512,1024]{0,1:T(8,128)}), f32[512,1024]{0,1:T(8,128)}) %all-reduce.4.cloned.1.call-update) | async-done | bytes 2097168 | tf_op jit(solution)/shard_map/psum | solution.py:12
  310.2 17.0 %convolution_subtract_fusion = f32[2048,1024]{0,1:T(8,128)S(1)} fusion(f32[2048,1024]{0,1:T(8,128)} %copy.22, f32[512,2048]{1,0:T(8,128)} %maximum_select_fusion, f32[512,1024]{0,1:T(8,128)} %all-reduce.4.cloned.1.call-done), kind=kOutput, calls=%fused_computation.9 | convolution fusion | flops 12886999040 | bytes 23068672 | tf_op jit(solution)/shard_map/dot_general | solution.py:16
  333.3 61.3 %all-gather.13.cloned.1.call-done = f32[128,1,2048]{2,1,0:T(1,128)} async-done(((f32[1,1,2048]{2,1,0:T(1,128)}), f32[128,1,2048]{2,1,0:T(1,128)}) %all-gather.13.cloned.1.call-update) | async-done | bytes 1048592 | tf_op jit(solution)/shard_map/all_gather | solution.py:46
  411.0 11.7 %cholesky.358 = f32[128,128]{1,0:T(8,128)S(1)} custom-call(f32[128,128]{1,0:T(8,128)S(1)} %cholesky.439), custom_call_target="Cholesky" | custom-call | tf_op jit(solution)/shard_map/jit(cholesky)/cholesky | solution.py:49
  422.8 9.8 %custom-call.31 = f32[1,128,128]{1,2,0:T(8,128)S(1)} custom-call(f32[1,128,128]{2,1,0:T(8,128)S(1)} %get-tuple-element.55), custom_call_target="InvertDiagBlocksLowerTriangular" | custom-call | tf_op jit(solution)/shard_map/jit(cholesky)/cholesky | solution.py:49
  433.3 11.7 %cholesky.377 = f32[128,128]{1,0:T(8,128)S(1)} custom-call(f32[128,128]{1,0:T(8,128)S(1)} %cholesky.443), custom_call_target="Cholesky" | custom-call | tf_op jit(solution)/shard_map/jit(cholesky)/cholesky | solution.py:49
  445.1 10.2 %custom-call.32 = f32[1,128,128]{1,2,0:T(8,128)S(1)} custom-call(f32[1,128,128]{2,1,0:T(8,128)S(1)} %get-tuple-element.52), custom_call_target="InvertDiagBlocksLowerTriangular" | custom-call | tf_op jit(solution)/shard_map/jit(cholesky)/cholesky | solution.py:49
  455.9 11.7 %cholesky.398 = f32[128,128]{1,0:T(8,128)S(1)} custom-call(f32[128,128]{1,0:T(8,128)S(1)} %cholesky.448), custom_call_target="Cholesky" | custom-call | tf_op jit(solution)/shard_map/jit(cholesky)/cholesky | solution.py:49
  467.7 9.8 %custom-call.33 = f32[1,128,128]{1,2,0:T(8,128)S(1)} custom-call(f32[1,128,128]{2,1,0:T(8,128)S(1)} %get-tuple-element.49), custom_call_target="InvertDiagBlocksLowerTriangular" | custom-call | tf_op jit(solution)/shard_map/jit(cholesky)/cholesky | solution.py:49
  478.1 11.7 %cholesky.415 = f32[128,128]{1,0:T(8,128)S(1)} custom-call(f32[128,128]{1,0:T(8,128)S(1)} %convolution_subtract_fusion.9), custom_call_target="Cholesky" | custom-call | tf_op jit(solution)/shard_map/jit(cholesky)/cholesky | solution.py:49
  502.7 39.3 %custom-call.34 = f32[4,128,128]{1,2,0:T(8,128)S(1)} custom-call(f32[4,128,128]{2,1,0:T(8,128)S(1)} %get-tuple-element.19), custom_call_target="InvertDiagBlocksLowerTriangular" | custom-call | tf_op jit(solution)/shard_map/jit(_solve_triangular)/triangular_solve | solution.py:52
  566.3 61.8 %all-reduce.6.cloned.1.call-done = f32[512,1024]{0,1:T(8,128)} async-done(((f32[512,1024]{0,1:T(8,128)}), f32[512,1024]{0,1:T(8,128)}) %all-reduce.6.cloned.1.call-update) | async-done | bytes 2097168 | tf_op jit(solution)/shard_map/psum | solution.py:12
  628.2 18.4 %subtract_select_fusion = f32[2048,1024]{0,1:T(8,128)} fusion(f32[2048,1024]{0,1:T(8,128)} %copy-done, pred[2048]{0:T(1024)(128)(4,1)S(1)} %broadcast_compare_fusion.1, pred[1024]{0:T(1024)(128)(4,1)S(1)} %fusion.86, f32[512,2048]{1,0:T(8,128)} %maximum_select_fusion.1, f32[512,1024]{0,1:T(8,128)} %all-reduce.6.cloned.1.call-done), kind=kOutput, calls=%fused_computation.6 | convolution fusion | flops 12891193344 | bytes 23071744 | tf_op jit(solution)/shard_map/dot_general | solution.py:16
  646.5 9.2 %copy.28 = f32[2048,1024]{1,0:T(8,128)} copy(f32[2048,1024]{0,1:T(8,128)} %subtract_select_fusion) | data formatting | bytes 16777216
  (131 shorter events, 129.0 us)
Async XLA Ops:
  7.2 69.7 %all-gather.11.cloned.1.call-start = ((), (), s32[]{:S(2)}) async-start(), calls=%async_computation.4 | async-start | bytes 1056768 | tf_op jit(solution)/shard_map/all_gather | solution.py:46
  8.7 215.4 %all-gather.7.cloned.1.call-start = ((), (), s32[]{:S(2)}) async-start(), calls=%async_computation | async-start | bytes 4456448 | tf_op jit(solution)/shard_map/all_gather | solution.py:51
  19.6 290.6 %all-reduce.4.cloned.1.call-start = ((), (), s32[]{:S(2)}) async-start(), calls=%async_computation.1 | async-start | bytes 4194304 | tf_op jit(solution)/shard_map/psum | solution.py:12
  224.1 5.7 copy-start.1
  246.5 148.0 %all-gather.13.cloned.1.call-start = ((), (), s32[]{:S(2)}) async-start(), calls=%async_computation.5 | async-start | bytes 1056768 | tf_op jit(solution)/shard_map/all_gather | solution.py:46
  327.2 3.4 copy-start
  331.5 210.6 %all-gather.9.cloned.1.call-start = ((), (), s32[]{:S(2)}) async-start(), calls=%async_computation.2 | async-start | bytes 4456448 | tf_op jit(solution)/shard_map/all_gather | solution.py:51
  333.2 295.0 %all-reduce.6.cloned.1.call-start = ((), (), s32[]{:S(2)}) async-start(), calls=%async_computation.3 | async-start | bytes 4194304 | tf_op jit(solution)/shard_map/psum | solution.py:12
  542.0 5.7 copy-start.2
Sparse Core Ops, SparseCore 0:
  10.8 65.9 all-gather.10
  79.5 49.2 all-gather.6
  246.6 63.5 all-reduce.3
  331.6 62.9 all-gather.12
  397.1 49.4 all-gather.8
  564.5 63.6 all-reduce.5
where the time goes:
time: 668 us; the launch traced here: 663 us
  other arithmetic  258 us (39%)
  waiting for transfers between devices  244 us (37%)
  local copies, waits for them, and re-layouts  78.7 us (12%)
  matrix products  61.3 us (9%)
  between operations  19.7 us (3%)
    another operation x29, other arithmetic, local(): lower_fac = jnp.linalg.cholesky(blocks)  158 us
    psum x2, waiting for transfers between devices, from_root(): return lax.psum(kept, axis)  125 us
    all_gather x2, waiting for transfers between devices, local(): blocks = lax.all_gather(flat_block, ('row', 'col'), axis=0, tiled=True)  118 us
    another operation x5, other arithmetic, local(): jax.scipy.linalg.solve_triangular(lower_fac, gathered, lower=True)  78.9 us
    dot_general x2, matrix products, outer_update(): lax.dot_general(left_fac, right_fac, (((0,), (0,)), ((), ())), precision=...  35.4 us
    unnamed x10, local copies, waits for them, and re-layouts  23.1 us
    another operation x14, matrix products, local(): jax.scipy.linalg.solve_triangular(lower_fac, gathered, lower=True)  22.2 us
    another operation x27, local copies, waits for them, and re-layouts, local(): jax.scipy.linalg.solve_triangular(lower_fac, gathered, lower=True)  15.5 us
  transfers between devices with their start and end apart: 6, of which 4 were waited for; matrix products, arithmetic and copies ran while one was open for 46% of the time, Pallas kernels for 0%

commit v1 on v0

v1 whole, which is shorter than its diff:
```python
import jax
import jax.numpy as jnp
from jax import lax
from jax.sharding import PartitionSpec as P

PANEL = 512
PANELS = 2
TILE = 32

HIGHEST = lax.Precision.HIGHEST


def mm(a, b):
    return jnp.dot(a, b, precision=HIGHEST, preferred_element_type=jnp.float32)


def mm_tn(a, b):
    return lax.dot_general(
        a, b, (((0,), (0,)), ((), ())), precision=HIGHEST, preferred_element_type=jnp.float32
    )


def mm_nt(a, b):
    return lax.dot_general(
        a, b, (((1,), (1,)), ((), ())), precision=HIGHEST, preferred_element_type=jnp.float32
    )


def tri_inverse(lower):
    eye = jnp.eye(lower.shape[0], dtype=lower.dtype)
    return jax.scipy.linalg.solve_triangular(lower, eye, lower=True)


def sym_chol(block):
    return jnp.linalg.cholesky(block)


def local(kernel):
    grid_rows = lax.axis_size("row")
    grid_cols = lax.axis_size("col")
    my_row = lax.axis_index("row")
    my_col = lax.axis_index("col")
    rows_loc, cols_loc = kernel.shape
    lead = PANELS * PANEL
    lead_rt = lead // (TILE * grid_rows)
    lead_ct = lead // (TILE * grid_cols)
    lead_r = lead_rt * TILE
    lead_c = lead_ct * TILE

    row_local = jnp.arange(rows_loc, dtype=jnp.int32)
    row_ids = (row_local // TILE * grid_rows + my_row) * TILE + row_local % TILE
    col_local = jnp.arange(cols_loc, dtype=jnp.int32)
    col_ids = (col_local // TILE * grid_cols + my_col) * TILE + col_local % TILE

    corner = kernel[:lead_r, :lead_c].reshape(1, lead_r * lead_c)
    blocks = lax.all_gather(corner, ("row", "col"), axis=0, tiled=True)
    blocks = blocks.reshape(grid_rows, grid_cols, lead_rt, TILE, lead_ct, TILE)
    a_lead = blocks.transpose(2, 0, 3, 4, 1, 5).reshape(lead, lead)

    cols_part = lax.all_gather(kernel[:, :lead_c], "col", axis=1, tiled=True)
    cols_part = cols_part.reshape(rows_loc, grid_cols, lead_ct, TILE)
    x_rows = cols_part.transpose(0, 2, 1, 3).reshape(rows_loc, lead)

    rows_part = lax.all_gather(kernel[:lead_r, :], "row", axis=0, tiled=True)
    rows_part = rows_part.reshape(grid_rows, lead_rt, TILE, cols_loc)
    y_cols = rows_part.transpose(1, 0, 2, 3).reshape(lead, cols_loc)

    a00 = a_lead[:PANEL, :PANEL]
    a01 = a_lead[:PANEL, PANEL:]
    a11 = a_lead[PANEL:, PANEL:]
    l0 = sym_chol(a00)
    l0inv = tri_inverse(l0)
    g0p1 = mm(l0inv, a01)
    s11 = a11 - mm_tn(g0p1, g0p1)
    l1 = sym_chol(s11)
    l1inv = tri_inverse(l1)

    def factor(panel_t, ids):
        g0 = mm(l0inv, panel_t[:PANEL])
        s1 = panel_t[PANEL:] - mm_tn(g0p1, g0)
        g1 = mm(l1inv, s1)
        g1 = jnp.where(ids[None, :] >= PANEL, g1, 0.0)
        return jnp.concatenate([g0, g1], axis=0)

    g_rows = factor(x_rows.T, row_ids)
    g_cols = factor(y_cols, col_ids)

    schur = kernel - mm_tn(g_rows, g_cols)
    keep = (row_ids[:, None] >= lead) & (col_ids[None, :] >= lead)
    trailing = jnp.where(keep, schur, 0.0)
    per_col = lead // grid_cols
    factor_out = lax.dynamic_slice_in_dim(g_rows, my_col * per_col, per_col, 0)
    return (trailing, factor_out)


def solution(mesh):
    return jax.shard_map(
        local,
        mesh=mesh,
        in_specs=(P("row", "col"),),
        out_specs=(P("row", "col"), P("col", "row")),
        check_vma=False,
    )
```

time: 668 us -> 592 us (0.89)
  waiting for transfers between devices: 244 us -> 97.9 us
  matrix products: 61.3 us -> 99.3 us
  local copies, waits for them, and re-layouts: 78.7 us -> 106 us
    psum x2 -> x0, waiting for transfers between devices: 125 us -> none  [from_root(): return lax.psum(kept, axis)]
    dot_general x2 -> x9, matrix products: 35.4 us -> 71.6 us  [the longest x4 45.8 us: mm_tn(): lax.dot_general(a, b, (((0,), (0,)), ((), ())), precision=HIGHEST, prefer...]
    all_gather x4 -> x3, waiting for transfers between devices: 118 us -> 97.9 us  [the longest x1 65 us: local(): blocks = lax.all_gather(corner, ('row', 'col'), axis=0, tiled=True)]
    unnamed x10 -> x28, local copies, waits for them, and re-layouts: 23.1 us -> 5.59 us
    reshape x6 -> x2, local copies, waits for them, and re-layouts: 13.6 us -> 30.8 us  [the longest x1 16.6 us: local(): blocks = blocks.reshape(grid_rows, grid_cols, lead_rt, TILE, lead_ct, TILE)]
    transpose x4 -> x2, local copies, waits for them, and re-layouts: 14.6 us -> 30.1 us  [the longest x1 26.1 us: local(): a_lead = blocks.transpose(2, 0, 3, 4, 1, 5).reshape(lead, lead)]
    select_n x4 -> x0, other arithmetic: 11.7 us -> none  [the longest x2 6.62 us: from_root(): jnp.where(lax.axis_index(axis) == source, value, 0).astype(value.dtype)]
    slice x3 -> x9, local copies, waits for them, and re-layouts: 0.92 us -> 12.1 us  [the longest x2 3.95 us: factor(): g0 = mm(l0inv, panel_t[:PANEL])]
  transfers between devices with their start and end apart: 6 -> 3, of which waited for: 4 -> 2; matrix products, arithmetic and copies ran while one was open for 46% -> 69% of each run, Pallas kernels for 0% -> 0%
where the time goes in v1:
time: 592 us; the launch traced here: 584 us
  other arithmetic  260 us (44%)
  local copies, waits for them, and re-layouts  106 us (18%)
  matrix products  99.3 us (17%)
  waiting for transfers between devices  97.9 us (17%)
  between operations  19.9 us (3%)
    another operation x29, other arithmetic, sym_chol(): return jnp.linalg.cholesky(block)  160 us
    another operation x5, other arithmetic, tri_inverse(): return jax.scipy.linalg.solve_triangular(lower, eye, lower=True)  82.9 us
    all_gather x1, waiting for transfers between devices, local(): blocks = lax.all_gather(corner, ('row', 'col'), axis=0, tiled=True)  65 us
    dot_general x4, matrix products, mm_tn(): lax.dot_general(a, b, (((0,), (0,)), ((), ())), precision=HIGHEST, prefer...  45.8 us
    all_gather x1, waiting for transfers between devices, local(): rows_part = lax.all_gather(kernel[:lead_r, :], 'row', axis=0, tiled=True)  32.9 us
    transpose x1, local copies, waits for them, and re-layouts, local(): a_lead = blocks.transpose(2, 0, 3, 4, 1, 5).reshape(lead, lead)  26.1 us
    dot_general x5, matrix products, mm(): return jnp.dot(a, b, precision=HIGHEST, preferred_element_type=jnp.float32)  25.8 us
    another operation x27, local copies, waits for them, and re-layouts, tri_inverse(): return jax.scipy.linalg.solve_triangular(lower, eye, lower=True)  23.6 us
  transfers between devices with their start and end apart: 3, of which 2 were waited for; matrix products, arithmetic and copies ran while one was open for 69% of the time, Pallas kernels for 0%

profile of v1, /device:TPU:0, one launch (start us, length us, event | category | flops | bytes accessed | tf_op | source)
XLA Modules:
  0.0 583.7 jit_solution(12073595241916444088)
XLA Ops:
  12.2 32.9 %all-gather.7.cloned.1.call-done = f32[1024,1024]{1,0:T(8,128)} async-done(((f32[128,1024]{1,0:T(8,128)}), f32[1024,1024]{1,0:T(8,128)}) %all-gather.7.cloned.1.call-update) | async-done | bytes 4194320 | tf_op jit(solution)/shard_map/all_gather | solution.py:64
  50.6 65.0 %all-gather.9.cloned.1.call-done = f32[128,1,8192]{2,1,0:T(1,128)} async-done(((f32[1,1,8192]{2,1,0:T(1,128)}), f32[128,1,8192]{2,1,0:T(1,128)}) %all-gather.9.cloned.1.call-update) | async-done | bytes 4194320 | tf_op jit(solution)/shard_map/all_gather | solution.py:56
  115.5 13.2 %reduce.16 = f32[128,8192]{1,0:T(8,128)} reduce(f32[128,1,8192]{2,1,0:T(1,128)} %all-gather.9.cloned.1.call-done, f32[]{:T(128)} %constant.211), dimensions={1}, to_apply=%all-gather.reduce_sub_computation | reduce | bytes 8388612 | tf_op jit(solution)/shard_map/all_gather | solution.py:56
  128.8 16.6 %reshape.139 = f32[8,16,4,32,2,32]{5,4,3,2,1,0:T(2,128)} reshape(f32[128,8192]{1,0:T(8,128)} %reduce.16) | data formatting | bytes 8388608 | tf_op jit(solution)/shard_map/reshape | solution.py:57
  145.4 26.1 %copy.20 = f32[4,8,32,2,16,32]{2,1,0,5,4,3:T(8,128)} copy(f32[4,8,32,2,16,32]{5,3,2,0,4,1:T(2,128)} %bitcast.121) | data formatting | bytes 8388608 | tf_op jit(solution)/shard_map/transpose | solution.py:58
  171.4 14.2 %reshape.140 = f32[1024,1024]{0,1:T(8,128)} reshape(f32[4,8,32,2,16,32]{2,1,0,5,4,3:T(8,128)} %copy.20) | data formatting | bytes 8388608 | tf_op jit(solution)/shard_map/reshape | solution.py:58
  191.9 11.7 %cholesky.286 = f32[128,128]{1,0:T(8,128)S(1)} custom-call(f32[128,128]{1,0:T(8,128)S(1)} %cholesky.426), custom_call_target="Cholesky" | custom-call | tf_op jit(solution)/shard_map/jit(cholesky)/cholesky | solution.py:35
  203.7 9.8 %custom-call.27 = f32[1,128,128]{1,2,0:T(8,128)S(1)} custom-call(f32[1,128,128]{2,1,0:T(8,128)S(1)} %get-tuple-element.61), custom_call_target="InvertDiagBlocksLowerTriangular" | custom-call | tf_op jit(solution)/shard_map/jit(cholesky)/cholesky | solution.py:35
  216.1 11.7 %cholesky.305 = f32[128,128]{1,0:T(8,128)S(1)} custom-call(f32[128,128]{1,0:T(8,128)S(1)} %cholesky.430), custom_call_target="Cholesky" | custom-call | tf_op jit(solution)/shard_map/jit(cholesky)/cholesky | solution.py:35
  227.9 10.0 %custom-call.28 = f32[1,128,128]{1,2,0:T(8,128)S(1)} custom-call(f32[1,128,128]{2,1,0:T(8,128)S(1)} %get-tuple-element.58), custom_call_target="InvertDiagBlocksLowerTriangular" | custom-call | tf_op jit(solution)/shard_map/jit(cholesky)/cholesky | solution.py:35
  239.4 11.7 %cholesky.326 = f32[128,128]{1,0:T(8,128)S(1)} custom-call(f32[128,128]{1,0:T(8,128)S(1)} %cholesky.435), custom_call_target="Cholesky" | custom-call | tf_op jit(solution)/shard_map/jit(cholesky)/cholesky | solution.py:35
  251.2 9.8 %custom-call.29 = f32[1,128,128]{1,2,0:T(8,128)S(1)} custom-call(f32[1,128,128]{2,1,0:T(8,128)S(1)} %get-tuple-element.55), custom_call_target="InvertDiagBlocksLowerTriangular" | custom-call | tf_op jit(solution)/shard_map/jit(cholesky)/cholesky | solution.py:35
  262.4 11.7 %cholesky.343 = f32[128,128]{1,0:T(8,128)S(1)} custom-call(f32[128,128]{1,0:T(8,128)S(1)} %convolution_subtract_fusion.12), custom_call_target="Cholesky" | custom-call | tf_op jit(solution)/shard_map/jit(cholesky)/cholesky | solution.py:35
  280.4 12.0 %while.4 = (s32[]{:T(128)}, f32[512,512]{1,0:T(8,128)}, s32[4,2]{0,1:T(2,128)S(1)}, f32[4,128,128]{2,1,0:T(8,128)S(1)}, s32[]{:T(128)}) while((s32[]{:T(128)}, f32[512,512]{1,0:T(8,128)}, s32[4,2]{0,1:T(2,128)S(1)}, f32[4,128,128]{2,1,0:T(8,128)S(1)}, s32[]{:T(128)}) %tuple.58), condition=%wide.while_cond, body=%wide.while_body.sunk | while | flops 2 | bytes 131181 | solution.py:31
  292.4 39.3 %custom-call.30 = f32[4,128,128]{1,2,0:T(8,128)S(1)} custom-call(f32[4,128,128]{2,1,0:T(8,128)S(1)} %get-tuple-element.18), custom_call_target="InvertDiagBlocksLowerTriangular" | custom-call | tf_op jit(solution)/shard_map/jit(_solve_triangular)/triangular_solve | solution.py:31
  347.9 11.7 %cholesky.358 = f32[128,128]{1,0:T(8,128)S(1)} custom-call(f32[128,128]{1,0:T(8,128)S(1)} %cholesky.439), custom_call_target="Cholesky" | custom-call | tf_op jit(solution)/shard_map/jit(cholesky)/cholesky | solution.py:35
  360.7 10.0 %custom-call.31 = f32[1,128,128]{1,2,0:T(8,128)S(1)} custom-call(f32[1,128,128]{2,1,0:T(8,128)S(1)} %get-tuple-element.51), custom_call_target="InvertDiagBlocksLowerTriangular" | custom-call | tf_op jit(solution)/shard_map/jit(cholesky)/cholesky | solution.py:35
  373.9 11.7 %cholesky.377 = f32[128,128]{1,0:T(8,128)S(1)} custom-call(f32[128,128]{1,0:T(8,128)S(1)} %cholesky.443), custom_call_target="Cholesky" | custom-call | tf_op jit(solution)/shard_map/jit(cholesky)/cholesky | solution.py:35
  398.4 11.7 %cholesky.398 = f32[128,128]{1,0:T(8,128)S(1)} custom-call(f32[128,128]{1,0:T(8,128)S(1)} %cholesky.448), custom_call_target="Cholesky" | custom-call | tf_op jit(solution)/shard_map/jit(cholesky)/cholesky | solution.py:35
  410.8 10.0 %custom-call.33 = f32[1,128,128]{1,2,0:T(8,128)S(1)} custom-call(f32[1,128,128]{2,1,0:T(8,128)S(1)} %get-tuple-element.45), custom_call_target="InvertDiagBlocksLowerTriangular" | custom-call | tf_op jit(solution)/shard_map/jit(cholesky)/cholesky | solution.py:35
  423.0 11.7 %cholesky.415 = f32[128,128]{1,0:T(8,128)S(1)} custom-call(f32[128,128]{1,0:T(8,128)S(1)} %convolution_subtract_fusion.11), custom_call_target="Cholesky" | custom-call | tf_op jit(solution)/shard_map/jit(cholesky)/cholesky | solution.py:35
  443.1 11.7 %while.5 = (s32[]{:T(128)}, f32[512,512]{1,0:T(8,128)}, s32[4,2]{0,1:T(2,128)S(1)}, f32[4,128,128]{2,1,0:T(8,128)S(1)}, s32[]{:T(128)}) while((s32[]{:T(128)}, f32[512,512]{1,0:T(8,128)}, s32[4,2]{0,1:T(2,128)S(1)}, f32[4,128,128]{2,1,0:T(8,128)S(1)}, s32[]{:T(128)}) %tuple.70), condition=%wide.while_cond.clone, body=%wide.while_body.clone.sunk | while | flops 2 | bytes 131181 | solution.py:31
  454.8 39.7 %custom-call.34 = f32[4,128,128]{1,2,0:T(8,128)S(1)} custom-call(f32[4,128,128]{2,1,0:T(8,128)S(1)} %get-tuple-element.19), custom_call_target="InvertDiagBlocksLowerTriangular" | custom-call | tf_op jit(solution)/shard_map/jit(_solve_triangular)/triangular_solve | solution.py:31
  545.2 31.7 %subtract_select_fusion = f32[2048,1024]{1,0:T(8,128)} fusion(f32[2048,1024]{1,0:T(8,128)} %param.4, pred[1024]{0:T(1024)(128)(4,1)S(1)} %get-tuple-element.67, pred[2048]{0:T(1024)(128)(4,1)S(1)} %get-tuple-element.69, f32[512,1024]{1,0:T(8,128)S(1)} %copy-done.11, f32[512,1024]{1,0:T(8,128)S(1)} %copy-done.3, f32[512,2048]{1,0:T(8,128)S(1)} %fusion.7, ...), kind=kOutput, calls=%fused_computation.8 | convolution fusion | flops 25779240960 | bytes 29363200 | tf_op jit(solution)/shard_map/dot_general | solution.py:18
  (140 shorter events, 141.8 us)
Async XLA Ops:
  7.2 3.7 slice-start
  7.2 38.0 %all-gather.7.cloned.1.call-start = ((), (), s32[]{:S(2)}) async-start(), calls=%async_computation.1 | async-start | bytes 4718592 | tf_op jit(solution)/shard_map/all_gather | solution.py:64
  9.2 106.3 %all-gather.9.cloned.1.call-start = ((), (), s32[]{:S(2)}) async-start(), calls=%async_computation.2 | async-start | bytes 4227072 | tf_op jit(solution)/shard_map/all_gather | solution.py:56
  10.8 505.8 %all-gather.5.cloned.1.call-start = ((), (), s32[]{:S(2)}) async-start(), calls=%async_computation | async-start | bytes 8912896 | tf_op jit(solution)/shard_map/all_gather | solution.py:60
  190.9 1.0 copy-start.10
  331.7 6.0 %copy-start = (f32[1024,1024]{0,1:T(8,128)S(1)}, f32[1024,1024]{0,1:T(8,128)}, u32[]{:S(2)}) copy-start(f32[1024,1024]{0,1:T(8,128)} %reshape.140) | copy-start | bytes 12582916
  337.8 7.3 %copy-start.7 = (f32[128,512]{1,0:T(8,128)}, f32[128,512]{1,0:T(8,128)S(1)}, u32[]{:S(2)}) copy-start(f32[128,512]{1,0:T(8,128)S(1)} %fusion.59) | copy-start | bytes 786436
  346.9 1.0 copy-start.9
  494.6 0.7 copy-start.12
  494.6 8.9 %copy-start.4 = (f32[2,8,32,1024]{3,2,1,0:T(8,128)S(1)}, f32[2,8,32,1024]{3,2,1,0:T(8,128)}, u32[]{:S(2)}) copy-start(f32[2,8,32,1024]{3,2,1,0:T(8,128)} %copy.26) | copy-start | bytes 6291460
  499.1 8.9 %copy-start.1 = (f32[2,8,32,1024]{3,2,1,0:T(8,128)S(1)}, f32[2,8,32,1024]{3,2,1,0:T(8,128)}, u32[]{:S(2)}) copy-start(f32[2,8,32,1024]{3,2,1,0:T(8,128)} %copy.27) | copy-start | bytes 6291460
  500.5 11.1 %copy-start.5 = (f32[128,512]{1,0:T(8,128)}, f32[128,512]{1,0:T(8,128)S(1)}, u32[]{:S(2)}) copy-start(f32[128,512]{1,0:T(8,128)S(1)} %fusion.54) | copy-start | bytes 786436
  508.0 3.5 copy-start.2
  516.7 4.0 copy-start.8
  527.8 7.8 %copy-start.6 = (f32[128,512]{1,0:T(8,128)S(1)}, f32[128,512]{1,0:T(8,128)}, u32[]{:S(2)}) copy-start(f32[128,512]{1,0:T(8,128)} %copy-done.5) | copy-start | bytes 786436
  542.8 1.8 copy-start.3
  542.8 2.4 copy-start.11
Sparse Core Ops, SparseCore 0:
  10.3 34.7 all-gather.6
  48.8 66.6 all-gather.8
  117.7 68.0 all-gather.4
